TPU v7x, 512 devices: a whole 4x8x8 slice. The times are simulated.
512 devices in a mesh: dp: 32 (over y_hi, x, core), tensor: 16 (over z, y_lo).
Axes of the slice: x: 4, y: 8 (y_hi: 4, y_lo: 2; y = y_hi * 2 + y_lo), z: 8, core: 2. Of those that a mesh axis runs over, the one named last changes fastest.
Arguments:
- tokens: bfloat16 [12288, 2048], P('dp'), may hold values from -6 to 6
- out_grad: bfloat16 [12288, 7168], P('dp', 'tensor'), may hold values from -6 to 6
- gate_weight: bfloat16 [2048, 7168], P('dp', 'tensor'), may hold values from -0.1875 to 0.1875
- up_weight: bfloat16 [2048, 7168], P('dp', 'tensor'), may hold values from -0.1875 to 0.1875
- gate_mask: int32 [32, 112], P('dp', 'tensor'), may hold values 0 or 1
- up_mask: int32 [32, 112], P('dp', 'tensor'), may hold values 0 or 1
Outputs:
- hidden: float32 [12288, 7168], P('dp', 'tensor')
- grad_tokens: bfloat16 [12288, 2048], P('dp')
- grad_gate: float32 [2048, 7168], P('dp', 'tensor')
- grad_up: float32 [2048, 7168], P('dp', 'tensor')
All inputs are finite; a program needn't handle non-finite values. No bound on the sum of `gate_mask` or of `up_mask` on one device may be relied on, other than what follows from the above.
Results may differ from a plain program's by a relative error of at most 0.014.
Values may be sent and summed in bfloat16 or wider, within the bound.
No kernel may reach another device: no remote copies, remote signals or barrier semaphores. Data moves between devices by JAX's collectives and lax.ppermute only.
A program may use at most 64 MiB of HBM per device.

v0:
```python
import jax
import jax.numpy as jnp
from jax import lax
from jax.sharding import PartitionSpec as P

BLOCK = 64


def expand(block_mask):
    height, breadth = block_mask.shape
    values = block_mask.astype(jnp.float32)
    return jnp.broadcast_to(values[:, None, :, None], (height, BLOCK, breadth, BLOCK)).reshape(
        height * BLOCK, breadth * BLOCK
    )


def local(tokens, out_grad, gate_weight, up_weight, gate_mask, up_mask):
    gate_keep = expand(gate_mask)
    up_keep = expand(up_mask)
    gate_eff = gate_weight * gate_keep.astype(jnp.bfloat16)
    up_eff = up_weight * up_keep.astype(jnp.bfloat16)
    local_both = jnp.concatenate([gate_eff, up_eff], axis=1)
    hidden_width = gate_weight.shape[1]
    gathered = lax.all_gather(local_both, "dp", axis=0, tiled=True)
    preact = jnp.dot(tokens, gathered, preferred_element_type=jnp.float32)
    gate = preact[:, :hidden_width]
    up = preact[:, hidden_width:]
    sigmoid_gate = jax.nn.sigmoid(gate)
    activation = gate * sigmoid_gate
    hidden = activation * up
    grad_float = out_grad.astype(jnp.float32)
    d_gate = (grad_float * up * sigmoid_gate * (1.0 + gate * (1.0 - sigmoid_gate))).astype(
        jnp.bfloat16
    )
    d_up = (grad_float * activation).astype(jnp.bfloat16)
    d_both = jnp.concatenate([d_gate, d_up], axis=1)
    partial_input = lax.dot_general(
        d_both, gathered, (((1,), (1,)), ((), ())), preferred_element_type=jnp.float32
    )
    grad_tokens = lax.psum(partial_input, "tensor").astype(jnp.bfloat16)
    summed = lax.psum_scatter(
        lax.dot_general(
            tokens, d_both, (((0,), (0,)), ((), ())), preferred_element_type=jnp.float32
        ).astype(jnp.bfloat16),
        "dp",
        scatter_dimension=0,
        tiled=True,
    ).astype(jnp.float32)
    grad_gate = summed[:, :hidden_width] * gate_keep
    grad_up = summed[:, hidden_width:] * up_keep
    return (hidden, grad_tokens, grad_gate, grad_up)


def solution(mesh):
    placed = (
        P("dp", None),
        P("dp", "tensor"),
        P("dp", "tensor"),
        P("dp", "tensor"),
        P("dp", "tensor"),
        P("dp", "tensor"),
    )
    return jax.shard_map(
        local,
        mesh=mesh,
        in_specs=placed,
        out_specs=(P("dp", "tensor"), P("dp", None), P("dp", "tensor"), P("dp", "tensor")),
        check_vma=False,
    )
```

profile of v0, /device:TPU:2, one launch (start us, length us, event | category | flops | bytes accessed | tf_op | source)
XLA Modules:
  0.0 270.0 jit_solution(18201012500881110290)
XLA Ops:
  7.2 0.0 copy-start
  7.2 0.0 all-gather.2.cloned.1.call-start
  7.2 0.8 convert_bitcast_fusion.2
  8.0 0.7 convert_bitcast_fusion.1
  8.7 0.1 broadcast_in_dim.33
  8.7 0.1 broadcast_in_dim.34
  8.8 0.1 broadcast_in_dim.29
  8.9 0.1 broadcast_in_dim.30
  9.0 0.9 broadcast_multiply_fusion
  9.9 0.7 pad_maximum_fusion.3
  10.6 0.0 all-gather.2.cloned.1.call-update
  10.6 0.0 copy-start.1
  10.6 0.0 reduce-scatter.4.cloned.1.call-start
  10.7 69.7 %all-gather.2.cloned.1.call-done = bf16[2048,896]{1,0:T(8,128)(2,1)} async-done(((bf16[64,896]{1,0:T(8,128)(2,1)}), bf16[2048,896]{1,0:T(8,128)(2,1)}) %all-gather.2.cloned.1.call-update) | async-done | bytes 3670032 | tf_op jit(solution)/shard_map/all_gather | solution.py:24
  80.3 0.0 copy-done
  80.3 4.1 %convolution_bitcast_fusion = f32[384,896]{0,1:T(8,128)S(1)} fusion(bf16[2048,896]{1,0:T(8,128)(2,1)} %all-gather.2.cloned.1.call-done, bf16[384,2048]{1,0:T(8,128)(2,1)S(1)} %copy-done), kind=kOutput, calls=%fused_computation.1 | convolution fusion | flops 1409286144 | bytes 6619136 | tf_op jit(solution)/shard_map/dot_general | solution.py:25
  84.5 0.0 copy-done.1
  84.5 1.3 fusion.2
  85.7 4.0 %convert_bitcast_fusion = bf16[2048,896]{0,1:T(8,128)(2,1)} fusion(bf16[384,2048]{1,0:T(8,128)(2,1)S(1)} %copy-done, bf16[384,448]{0,1:T(8,128)(2,1)S(1)} %get-tuple-element.13, bf16[384,448]{0,1:T(8,128)(2,1)S(1)} %get-tuple-element.12), kind=kOutput, calls=%fused_computation | convolution fusion | flops 1412497408 | bytes 5931008 | tf_op jit(solution)/shard_map/dot_general | solution.py:42
  89.7 6.1 %copy.14 = bf16[2048,896]{1,0:T(8,128)(2,1)} copy(bf16[2048,896]{0,1:T(8,128)(2,1)} %convert_bitcast_fusion) | data formatting | bytes 7340032
  95.8 0.0 reduce-scatter.4.cloned.1.call-update
  95.8 5.6 %fusion.5 = f32[384,2048]{1,0:T(8,128)} fusion(bf16[2048,896]{1,0:T(8,128)(2,1)} %all-gather.2.cloned.1.call-done, bf16[384,448]{0,1:T(8,128)(2,1)S(1)} %get-tuple-element.13, bf16[384,448]{0,1:T(8,128)(2,1)S(1)} %get-tuple-element.12), kind=kOutput, calls=%fused_computation.12 | convolution fusion | flops 1410662400 | bytes 7503872 | tf_op jit(solution)/shard_map/dot_general | solution.py:37
  101.4 158.8 %all-reduce.1 = bf16[384,2048]{1,0:T(8,128)(2,1)} all-reduce(f32[384,2048]{1,0:T(8,128)} %fusion.5), channel_id=1, replica_groups=mesh['dp'=32,'tensor'=16] {'tensor'}, use_global_device_ids=true, to_apply=%region_0.0 | all-reduce | flops 786432 | bytes 4718592 | tf_op jit(solution)/shard_map/psum | solution.py:40
  260.3 0.0 reduce-scatter.4.cloned.1.call-done
  260.3 1.1 copy.15
  261.4 0.2 slice_multiply_fusion.1
  261.6 0.8 copy.13
  262.4 0.8 copy.12
  (3 shorter events, 0.0 us)
Async XLA Ops:
  7.2 73.2 %copy-start = (bf16[384,2048]{1,0:T(8,128)(2,1)S(1)}, bf16[384,2048]{1,0:T(8,128)(2,1)}, u32[]{:S(2)}) copy-start(bf16[384,2048]{1,0:T(8,128)(2,1)} %param.6) | copy-start | bytes 4718596
  7.2 73.1 %all-gather.2.cloned.1.call-start = ((), (), s32[]{:S(2)}) async-start(), calls=%async_computation.1 | async-start | bytes 3784704 | tf_op jit(solution)/shard_map/all_gather | solution.py:24
  10.6 73.9 %copy-start.1 = (bf16[384,448]{0,1:T(8,128)(2,1)S(1)}, bf16[384,448]{0,1:T(8,128)(2,1)}, u32[]{:S(2)}) copy-start(bf16[384,448]{0,1:T(8,128)(2,1)} %param.7) | copy-start | bytes 1032196
  10.6 249.7 %reduce-scatter.4.cloned.1.call-start = ((), (), s32[]{:S(2)}) async-start(), calls=%async_computation.2 | async-start | bytes 3784704
Sparse Core Ops, SparseCore 0:
  11.7 68.5 all-gather.1
  96.0 108.4 reduce-scatter.3
where the time goes:
time: 270 us
  blocking collectives  159 us (59%)
  waiting for transfers between devices  69.7 us (26%)
  between operations  14.1 us (5%)
  matrix products  13.7 us (5%)
  local copies, waits for them, and re-layouts  8.99 us (3%)
  other arithmetic  4.54 us (2%)
    psum x1, blocking collectives, local(): grad_tokens = lax.psum(partial_input, 'tensor').astype(jnp.bfloat16)  159 us
    all_gather x1, waiting for transfers between devices, local(): gathered = lax.all_gather(local_both, 'dp', axis=0, tiled=True)  69.7 us
    unnamed x8, local copies, waits for them, and re-layouts  8.7 us
    dot_general x1, matrix products, local(): lax.dot_general(d_both, gathered, (((1,), (1,)), ((), ())), preferred_ele...  5.62 us
  transfers between devices with their start and end apart: 2, of which 1 were waited for; matrix products, arithmetic and copies ran while one was open for 2% of the time, Pallas kernels for 0%

commit v1 on v0

--- a/solution.py
+++ b/solution.py
@@ -21,7 +21,8 @@
     up_eff = up_weight * up_keep.astype(jnp.bfloat16)
     local_both = jnp.concatenate([gate_eff, up_eff], axis=1)
     hidden_width = gate_weight.shape[1]
-    gathered = lax.all_gather(local_both, "dp", axis=0, tiled=True)
+    sent = jnp.stack([local_both] * lax.axis_size("dp"))
+    gathered = jnp.concatenate(lax.all_to_all(sent, "dp", 0, 0), axis=0)
     preact = jnp.dot(tokens, gathered, preferred_element_type=jnp.float32)
     gate = preact[:, :hidden_width]
     up = preact[:, hidden_width:]

time: 270 us -> 297 us (1.10)
  the two profiles are of different devices: /device:TPU:2 before, /device:TPU:16 now
where the time goes in v1:
time: 297 us
  blocking collectives  257 us (87%)
  between operations  14.1 us (5%)
  matrix products  11.7 us (4%)
  local copies, waits for them, and re-layouts  9.52 us (3%)
  other arithmetic  3.88 us (1%)
    psum x1, blocking collectives, local(): grad_tokens = lax.psum(partial_input, 'tensor').astype(jnp.bfloat16)  162 us
    all_to_all x1, blocking collectives, local(): gathered = jnp.concatenate(lax.all_to_all(sent, 'dp', 0, 0), axis=0)  95.1 us
    unnamed x10, local copies, waits for them, and re-layouts  8.71 us
  transfers between devices with their start and end apart: 1, of which 0 were waited for; matrix products, arithmetic and copies ran while one was open for 2% of the time, Pallas kernels for 0%

profile of v1, /device:TPU:16, one launch (start us, length us, event | category | flops | bytes accessed | tf_op | source)
XLA Modules:
  0.0 296.5 jit_solution(5327391517222812875)
XLA Ops:
  7.2 0.0 copy-start
  7.2 0.0 reduce-scatter.4.cloned.1.call-start
  7.2 0.8 convert_bitcast_fusion.2
  8.0 0.7 convert_bitcast_fusion.1
  8.7 0.1 broadcast_in_dim.33
  8.7 0.1 broadcast_in_dim.34
  8.8 0.1 broadcast_in_dim.29
  8.9 0.1 broadcast_in_dim.30
  9.0 0.9 broadcast_multiply_fusion
  9.9 0.1 pad_maximum_fusion.3
  9.9 0.5 stack.2
  10.5 95.1 %all_to_all.5 = bf16[32,64,896]{2,1,0:T(8,128)(2,1)S(1)} all-to-all(bf16[32,64,896]{2,1,0:T(8,128)(2,1)S(1)} %stack.2), channel_id=1, replica_groups=mesh['dp'=32,'tensor'=16] {'dp'}, dimensions={0} | all-to-all | bytes 7340032 | tf_op jit(solution)/shard_map/all_to_all | solution.py:25
  105.6 0.0 copy-start.1
  105.6 0.0 copy-done
  105.6 0.0 copy-start.2
  105.6 2.1 convolution_bitcast_fusion
  107.7 0.0 copy-done.1
  107.7 0.0 copy-done.2
  107.7 1.3 fusion.2
  109.0 4.0 %convert_bitcast_fusion = bf16[2048,896]{0,1:T(8,128)(2,1)} fusion(bf16[384,2048]{1,0:T(8,128)(2,1)S(1)} %copy-done, bf16[384,448]{0,1:T(8,128)(2,1)S(1)} %get-tuple-element.13, bf16[384,448]{0,1:T(8,128)(2,1)S(1)} %get-tuple-element.12), kind=kOutput, calls=%fused_computation | convolution fusion | flops 1412497408 | bytes 5931008 | tf_op jit(solution)/shard_map/dot_general | solution.py:43
  112.9 6.1 %copy.14 = bf16[2048,896]{1,0:T(8,128)(2,1)} copy(bf16[2048,896]{0,1:T(8,128)(2,1)} %convert_bitcast_fusion) | data formatting | bytes 7340032
  119.0 0.0 reduce-scatter.4.cloned.1.call-update
  119.1 5.6 %fusion.5 = f32[384,2048]{1,0:T(8,128)} fusion(bf16[2048,896]{1,0:T(8,128)(2,1)} %bitcast.15, bf16[384,448]{0,1:T(8,128)(2,1)S(1)} %get-tuple-element.13, bf16[384,448]{0,1:T(8,128)(2,1)S(1)} %get-tuple-element.12), kind=kOutput, calls=%fused_computation.12 | convolution fusion | flops 1410662400 | bytes 7503872 | tf_op jit(solution)/shard_map/dot_general | solution.py:38
  124.6 162.2 %all-reduce.1 = bf16[384,2048]{1,0:T(8,128)(2,1)} all-reduce(f32[384,2048]{1,0:T(8,128)} %fusion.5), channel_id=1, replica_groups=mesh['dp'=32,'tensor'=16] {'tensor'}, use_global_device_ids=true, to_apply=%region_0.0 | all-reduce | flops 786432 | bytes 4718592 | tf_op jit(solution)/shard_map/psum | solution.py:41
  286.8 0.0 reduce-scatter.4.cloned.1.call-done
  286.8 1.1 copy.15
  288.0 0.2 slice_multiply_fusion.1
  288.1 0.8 copy.13
  288.9 0.8 copy.12
  (3 shorter events, 0.0 us)
Async XLA Ops:
  7.2 98.4 %copy-start = (bf16[384,2048]{1,0:T(8,128)(2,1)S(1)}, bf16[384,2048]{1,0:T(8,128)(2,1)}, u32[]{:S(2)}) copy-start(bf16[384,2048]{1,0:T(8,128)(2,1)} %param.6) | copy-start | bytes 4718596
  7.2 279.7 %reduce-scatter.4.cloned.1.call-start = ((), (), s32[]{:S(2)}) async-start(), calls=%async_computation.2 | async-start | bytes 3784704
  105.6 2.1 copy-start.1
  105.6 2.1 copy-start.2
Sparse Core Ops, SparseCore 0:
  119.2 109.8 reduce-scatter.3

commit v2 on v0

--- a/solution.py
+++ b/solution.py
@@ -4,6 +4,11 @@
 from jax.sharding import PartitionSpec as P
 
 BLOCK = 64
+
+
+def add_all(shard, axis):
+    parts = lax.all_gather(shard, axis)
+    return jnp.sum(parts, axis=0)
 
 
 def expand(block_mask):
@@ -37,7 +42,7 @@
     partial_input = lax.dot_general(
         d_both, gathered, (((1,), (1,)), ((), ())), preferred_element_type=jnp.float32
     )
-    grad_tokens = lax.psum(partial_input, "tensor").astype(jnp.bfloat16)
+    grad_tokens = add_all(partial_input, "tensor").astype(jnp.bfloat16)
     summed = lax.psum_scatter(
         lax.dot_general(
             tokens, d_both, (((0,), (0,)), ((), ())), preferred_element_type=jnp.float32

time: 270 us -> 1250 us (4.63)
  the two profiles are of different devices: /device:TPU:2 before, /device:TPU:1 now
where the time goes in v2:
time: 1250 us
  waiting for transfers between devices  1190 us (95%)
  other arithmetic  23.2 us (2%)
  between operations  13.8 us (1%)
  matrix products  13.6 us (1%)
    all_gather x1, waiting for transfers between devices, add_all(): parts = lax.all_gather(shard, axis)  1030 us
    unnamed x4, waiting for transfers between devices  95.4 us
    all_gather x1, waiting for transfers between devices, local(): gathered = lax.all_gather(local_both, 'dp', axis=0, tiled=True)  71 us
  transfers between devices with their start and end apart: 3, of which 3 were waited for; matrix products, arithmetic and copies ran while one was open for 1% of the time, Pallas kernels for 0%

profile of v2, /device:TPU:1, one launch (start us, length us, event | category | flops | bytes accessed | tf_op | source)
XLA Modules:
  0.0 1253.0 jit_solution(8944647205983194445)
XLA Ops:
  7.2 0.0 copy-start
  7.2 0.0 all-gather.4.cloned.1.call-start
  7.2 0.8 convert_bitcast_fusion.2
  8.0 0.7 convert_bitcast_fusion.1
  8.7 0.1 broadcast_in_dim.33
  8.7 0.1 broadcast_in_dim.34
  8.8 0.1 broadcast_in_dim.29
  8.9 0.1 broadcast_in_dim.30
  9.0 0.9 broadcast_multiply_fusion
  9.9 0.7 pad_maximum_fusion.3
  10.6 0.0 all-gather.4.cloned.1.call-update
  10.6 0.0 copy-start.2
  10.6 0.0 reduce-scatter.4.cloned.1.call-start
  10.7 71.0 %all-gather.4.cloned.1.call-done = bf16[2048,896]{1,0:T(8,128)(2,1)} async-done(((bf16[64,896]{1,0:T(8,128)(2,1)}), bf16[2048,896]{1,0:T(8,128)(2,1)}) %all-gather.4.cloned.1.call-update) | async-done | bytes 3670032 | tf_op jit(solution)/shard_map/all_gather | solution.py:29
  81.7 0.0 copy-done
  81.7 4.1 convolution_bitcast_fusion
  85.8 0.0 copy-done.2
  85.8 1.3 fusion.2
  87.1 3.9 convert_bitcast_fusion
  91.0 6.1 copy.14
  97.1 0.0 reduce-scatter.4.cloned.1.call-update
  97.1 0.0 all-gather.6.cloned.1.call-start
  97.2 5.6 fusion.5
  102.7 0.0 all-gather.6.cloned.1.call-update
  102.7 95.3 %reduce-scatter.4.cloned.1.call-done = bf16[64,896]{1,0:T(8,128)(2,1)} async-done(((bf16[2048,896]{1,0:T(8,128)(2,1)}), bf16[64,896]{1,0:T(8,128)(2,1)}) %reduce-scatter.4.cloned.1.call-update) | async-done | bytes 114704
  198.1 1.1 copy.15
  199.2 0.2 slice_multiply_fusion.1
  199.4 0.8 copy.13
  200.1 0.8 copy.12
  200.9 1026.9 %all-gather.6.cloned.1.call-done = f32[6144,2048]{1,0:T(8,128)} async-done(((f32[384,2048]{1,0:T(8,128)}), f32[6144,2048]{1,0:T(8,128)}) %all-gather.6.cloned.1.call-update) | async-done | bytes 50331664 | tf_op jit(solution)/shard_map/all_gather | solution.py:10
  1227.8 0.0 copy-start.1
  1227.8 18.6 %reduce_sum.9 = bf16[384,2048]{1,0:T(8,128)(2,1)} reduce(f32[16,384,2048]{2,1,0:T(8,128)} %bitcast.14, f32[]{:T(128)} %constant.1.clone.1), dimensions={0}, to_apply=%region_0.0 | reduce | flops 11796480 | bytes 51904516 | tf_op jit(solution)/shard_map/reduce_sum | solution.py:11
  1246.5 0.0 copy-done.1
  (3 shorter events, 0.0 us)
Async XLA Ops:
  7.2 74.5 %copy-start = (bf16[384,2048]{1,0:T(8,128)(2,1)S(1)}, bf16[384,2048]{1,0:T(8,128)(2,1)}, u32[]{:S(2)}) copy-start(bf16[384,2048]{1,0:T(8,128)(2,1)} %param.6) | copy-start | bytes 4718596
  7.2 74.5 %all-gather.4.cloned.1.call-start = ((), (), s32[]{:S(2)}) async-start(), calls=%async_computation.1 | async-start | bytes 3784704 | tf_op jit(solution)/shard_map/all_gather | solution.py:29
  10.6 75.2 %copy-start.2 = (bf16[384,448]{0,1:T(8,128)(2,1)S(1)}, bf16[384,448]{0,1:T(8,128)(2,1)}, u32[]{:S(2)}) copy-start(bf16[384,448]{0,1:T(8,128)(2,1)} %param.7) | copy-start | bytes 1032196
  10.6 187.4 %reduce-scatter.4.cloned.1.call-start = ((), (), s32[]{:S(2)}) async-start(), calls=%async_computation.3 | async-start | bytes 3784704
  97.1 1130.7 %all-gather.6.cloned.1.call-start = ((), (), s32[]{:S(2)}) async-start(), calls=%async_computation.2 | async-start | bytes 53477376 | tf_op jit(solution)/shard_map/all_gather | solution.py:10
  1227.8 18.6 %copy-start.1 = (bf16[384,2048]{1,0:T(8,128)(2,1)S(1)}, bf16[384,2048]{1,0:T(8,128)(2,1)}, u32[]{:S(2)}) copy-start(bf16[384,2048]{1,0:T(8,128)(2,1)} %param.6) | copy-start | bytes 4718596
Sparse Core Ops, SparseCore 0:
  11.7 69.9 all-gather.3
  97.2 100.7 reduce-scatter.3
  200.2 1027.6 all-gather.5
